TPU v7x, 256 devices: a whole 4x4x8 slice. The times are simulated.
256 devices in a mesh: slab: 64 (over x, z, core), img: 4 (over y).
Axes of the slice: x: 4, y: 4, z: 8, core: 2. Of those that a mesh axis runs over, the one named last changes fastest.
Arguments:
- volume: bfloat16 [32768, 256], P('slab'), may hold values from -6 to 6
- interp: bfloat16 [4, 64, 16, 32768], P('img', None, None, 'slab'), may hold values from -0.09375 to 0.09375
- block_index: int32 [4, 64, 64], P('img'), may hold values from 0 to 7
- images: bfloat16 [4, 1024, 128, 256], P('img', 'slab'), may hold values from -6 to 6
- defocus: float32 [4, 1024], P('img', 'slab'), may hold values from 5000 to 25000
- orient: int32 [4, 1024, 4], P('img', 'slab'), may hold values from 0 to 63, all different within a row
Outputs:
- update: float32 [32768, 256], P('slab')
- weights: float32 [4, 1024, 64], P('img', 'slab')
Inputs may be any that keep to these rules, and one draw needn't show every extreme that they name: `orient`: each image lists 4 different orientations of its group.
All inputs are finite; a program needn't handle non-finite values.
Results may differ from a plain program's by a relative error of at most 0.0077.
Values may be sent and summed in bfloat16 or wider, within the bound.
A program may use at most 64 MiB of HBM per device.

v0:
```python
import math
import jax
import jax.numpy as jnp
from jax import lax
from jax.sharding import PartitionSpec as P

BOX = 256
NS = 16
wave_length = 0.0197
aberration = 27000000.0
amplitude = 0.1
grid_side = 4


def phase_tables(fourier, shifts, box):
    freq = (jnp.arange(fourier, dtype=jnp.int32) - fourier // 2).astype(jnp.float32)
    shift_steps = jnp.arange(shifts, dtype=jnp.int32)
    shift_x = (2 * (shift_steps // grid_side) - (grid_side - 1)).astype(jnp.float32)
    shift_y = (2 * (shift_steps % grid_side) - (grid_side - 1)).astype(jnp.float32)
    angle = 2.0 * math.pi / box * (freq[:, None, None] * shift_x + freq[None, :, None] * shift_y)
    forward = jnp.stack([jnp.cos(angle), jnp.sin(angle)], axis=1).reshape(
        2 * fourier * fourier, shifts
    )
    backward = jnp.stack([jnp.cos(angle), -jnp.sin(angle)], axis=1).reshape(
        2 * fourier * fourier, shifts
    )
    return (forward.astype(jnp.bfloat16), backward.T.astype(jnp.bfloat16))


def contrast(defocus_blk, fourier, box):
    freq = (jnp.arange(fourier, dtype=jnp.int32) - fourier // 2).astype(jnp.float32)
    wave_sq = (freq[:, None] * freq[:, None] + freq[None, :] * freq[None, :]) / (box * box)
    phase = math.pi * wave_length * defocus_blk[:, None, None] * wave_sq
    phase = phase - 0.5 * math.pi * aberration * wave_length**3 * wave_sq * wave_sq
    return -(math.sqrt(1.0 - amplitude * amplitude) * jnp.sin(phase) + amplitude * jnp.cos(phase))


def correlate(panels, image_blk, list_blk, defocus_blk, phase_fwd, phase_back, box):
    count = image_blk.shape[0]
    fourier = image_blk.shape[1]
    picks = list_blk.shape[1]
    shifts = phase_fwd.shape[1]
    ctf = contrast(defocus_blk, fourier, box)
    weighted = ctf[:, :, None, :] * image_blk.astype(jnp.float32).reshape(
        count, fourier, 2, fourier
    )
    real_u = weighted[:, None, :, 0]
    imag_u = weighted[:, None, :, 1]
    chosen = panels[list_blk].astype(jnp.float32).reshape(count, picks, fourier, 2, fourier)
    real_p = chosen[:, :, :, 0]
    imag_p = chosen[:, :, :, 1]
    product = jnp.stack(
        [real_p * real_u + imag_p * imag_u, real_p * imag_u - imag_p * real_u], axis=3
    )
    product = product.astype(jnp.bfloat16).reshape(count * picks, 2 * fourier * fourier)
    scores = jnp.dot(product, phase_fwd, preferred_element_type=jnp.float32) / fourier
    scores = scores.reshape(count, picks * shifts)
    squared = scores * scores
    weights = squared / (jnp.mean(squared, axis=1, keepdims=True) + 1e-05)
    rounded = weights.astype(jnp.bfloat16).reshape(count * picks, shifts)
    spread = jnp.dot(rounded, phase_back, preferred_element_type=jnp.float32)
    spread = spread.reshape(count, picks, fourier, 2, fourier)
    real_e = spread[:, :, :, 0]
    imag_e = spread[:, :, :, 1]
    backed = jnp.stack(
        [real_u * real_e - imag_u * imag_e, real_u * imag_e + imag_u * real_e], axis=3
    )
    backed = backed.astype(jnp.bfloat16).reshape(count * picks, 2 * fourier * fourier)
    return (weights, backed)


def on_device(volume, interp, block_index, images, defocus, orient):
    slab_count = lax.axis_size("slab")
    slab_index = lax.axis_index("slab")
    orient_count = interp.shape[1]
    ori_dev = orient_count // slab_count
    block_rows = interp.shape[2]
    fourier = images.shape[2]
    block_count = fourier // block_rows
    img_dev = images.shape[1]
    picks = orient.shape[2]
    levels = jnp.arange(block_count, dtype=jnp.int32)
    partial_value = jnp.einsum("jpr,rx->jpx", interp[0], volume, preferred_element_type=jnp.float32)
    owned_idx = lax.dynamic_slice_in_dim(block_index[0], slab_index * ori_dev, ori_dev, 0)
    received = lax.all_to_all(
        partial_value.reshape(slab_count, ori_dev * block_rows, 2 * fourier),
        "slab",
        split_axis=0,
        concat_axis=0,
        tiled=True,
    ).reshape(slab_count, ori_dev, block_rows, 2 * fourier)
    place = (owned_idx[:, :, None] == levels).astype(jnp.float32)
    summed = jnp.einsum(
        "osb,sopx->obpx",
        place,
        received,
        precision=lax.Precision.HIGHEST,
        preferred_element_type=jnp.float32,
    ).reshape(ori_dev, fourier, 2 * fourier)
    panels = lax.all_gather(summed.astype(jnp.bfloat16), "slab", axis=0, tiled=True)
    phase_fwd, phase_back = phase_tables(fourier, NS, BOX)
    blk = math.gcd(img_dev, 32)
    blk_total = img_dev // blk

    def per_block(pieces):
        image_blk, list_blk, defocus_blk = pieces
        return correlate(panels, image_blk, list_blk, defocus_blk, phase_fwd, phase_back, BOX)

    weights, backs = lax.map(
        per_block,
        (
            images[0].reshape(blk_total, blk, fourier, 2 * fourier),
            orient[0].reshape(blk_total, blk, picks),
            defocus[0].reshape(blk_total, blk),
        ),
    )
    all_slices = backs.reshape(img_dev * picks, 2 * fourier * fourier)
    member = (
        orient[0].reshape(-1)[:, None] == jnp.arange(orient_count, dtype=jnp.int32)[None, :]
    ).astype(jnp.bfloat16)
    contrib = lax.dot_general(
        member, all_slices, (((0,), (0,)), ((), ())), preferred_element_type=jnp.float32
    ).reshape(orient_count, fourier, 2 * fourier)
    back_own = lax.psum_scatter(contrib, "slab", scatter_dimension=0, tiled=True).astype(
        jnp.bfloat16
    )
    back_own = back_own.reshape(ori_dev, block_count, block_rows, 2 * fourier)
    chosen_back = (owned_idx[:, :, None] == levels).astype(jnp.bfloat16)
    outgoing = jnp.einsum(
        "osb,obpx->sopx", chosen_back, back_own, preferred_element_type=jnp.float32
    )
    outgoing = outgoing.astype(jnp.bfloat16).reshape(slab_count * ori_dev, block_rows, 2 * fourier)
    incoming = lax.all_to_all(outgoing, "slab", split_axis=0, concat_axis=0, tiled=True)
    column = jnp.einsum("jpr,jpx->rx", interp[0], incoming, preferred_element_type=jnp.float32)
    summed_cols = lax.psum(column, "img")
    update = summed_cols / math.sqrt(img_dev * slab_count)
    return (update, weights)


def solution(mesh):
    return jax.shard_map(
        on_device,
        mesh=mesh,
        in_specs=(
            P("slab", None),
            P("img", None, None, "slab"),
            P("img", None, None),
            P("img", "slab", None, None),
            P("img", "slab"),
            P("img", "slab", None),
        ),
        out_specs=(P("slab", None), P("img", "slab", None)),
        check_vma=False,
    )
```

profile of v0, /device:TPU:2, one launch (start us, length us, event | category | flops | bytes accessed | tf_op | source)
XLA Modules:
  0.0 444.3 jit_solution(18430927952869716344)
XLA Ops:
  7.2 1.2 copy-done
  8.4 2.4 fusion.10
  10.8 12.0 %all-to-all-start = ((f32[64,16,256]{2,1,0:T(8,128)}), f32[64,16,256]{2,1,0:T(8,128)S(1)}, u32[]{:S(2)}, u32[]{:S(2)}) async-start(f32[64,16,256]{2,1,0:T(8,128)} %fusion.10), calls=%async_computation | async-start | bytes 2097152 | tf_op jit(solution)/shard_map/all_to_all | solution.py:85
  22.8 0.0 all-gather.2.cloned.1.call-start
  22.8 0.7 dynamic-slice_bitcast_fusion
  23.5 26.4 %all-to-all-done = f32[64,16,256]{2,1,0:T(8,128)S(1)} async-done(((f32[64,16,256]{2,1,0:T(8,128)}), f32[64,16,256]{2,1,0:T(8,128)S(1)}, u32[]{:S(2)}, u32[]{:S(2)}) %all-to-all-start) | async-done | bytes 1048608 | tf_op jit(solution)/shard_map/all_to_all | solution.py:85
  49.9 1.0 convolution_convert_fusion.1
  51.0 0.6 copy.62
  51.6 0.0 all-gather.2.cloned.1.call-update
  51.6 0.2 reduce-scatter.2.cloned.1.call-start
  51.9 0.1 copy.57
  52.0 0.1 copy.63
  52.0 0.1 reshape.434
  52.1 2.1 reshape.430
  54.3 0.1 broadcast_multiply_fusion.2
  54.3 0.1 copy.68
  54.4 5.4 %fusion.14 = (bf16[128,1,128,16]{2,3,1,0:T(8,128)(2,1)S(1)}, bf16[128,1,128,16]{2,3,1,0:T(8,128)(2,1)}, bf16[128,1,128,16]{2,3,1,0:T(8,128)(2,1)S(1)}) fusion(f32[128,16]{0,1:T(8,128)S(1)} %get-tuple-element.51, f32[128,16]{1,0:T(8,128)S(1)} %copy.68), kind=kLoop, calls=%fused_computation.32 | loop fusion | flops 1572864 | bytes 1589248 | tf_op jit(solution)/shard_map/convert.7
  59.8 0.8 copy-done.2
  60.6 0.1 pad_maximum_fusion.3
  60.7 1.9 copy.69
  62.6 2.6 convert_element_type.148
  65.2 0.1 eq.65
  65.4 0.1 add_multiply_fusion.2
  65.5 3.9 add_negate_fusion
  69.3 1.2 copy_multiply_fusion
  70.6 1.1 slice_bitcast_fusion.1
  71.7 56.5 %all-gather.2.cloned.1.call-done = bf16[64,128,256]{2,1,0:T(8,128)(2,1)} async-done(((bf16[1,128,256]{2,1,0:T(8,128)(2,1)}), bf16[64,128,256]{2,1,0:T(8,128)(2,1)}) %all-gather.2.cloned.1.call-update) | async-done | bytes 4194320 | tf_op jit(solution)/shard_map/all_gather | solution.py:100
  128.2 5.0 %gather_fusion = bf16[64,128,256]{2,1,0:T(8,128)(2,1)} fusion(bf16[64,128,256]{2,1,0:T(8,128)(2,1)} %all-gather.2.cloned.1.call-done, s32[1024]{0:T(1024)S(1)} %pad_clamp_fusion), kind=kCustom, calls=%fused_computation | custom fusion | bytes 8388864 | tf_op jit(solution)/shard_map/while/body/eval_jaxpr/gather | solution.py:49
  133.2 7.0 %copy.64 = f32[64,128,256]{1,2,0:T(8,128)} copy(bf16[64,128,256]{2,1,0:T(8,128)(2,1)} %gather_fusion) | data formatting | bytes 12582912 | tf_op jit(solution)/shard_map/while/body/eval_jaxpr/convert_element_type | solution.py:49
  140.2 7.8 %fusion.36 = (f32[16,4,128,1,128]{2,4,3,1,0:T(8,128)}, f32[16,4,128,1,128]{2,4,3,1,0:T(8,128)}) fusion(f32[16,4,128,2,128]{2,4,3,1,0:T(8,128)} %bitcast.62), kind=kLoop, calls=%fused_computation.73 | loop fusion | bytes 16777216 | tf_op jit(solution)/shard_map/while/body/eval_jaxpr/slice | solution.py:50
  148.0 5.5 %copy.84 = f32[16,4,128,1,128]{4,0,3,2,1:T(8,128)} copy(f32[16,4,128,1,128]{2,4,3,1,0:T(8,128)} %get-tuple-element.41) | data formatting | bytes 8388608
  153.4 5.5 %copy.85 = f32[16,4,128,1,128]{4,0,3,2,1:T(8,128)} copy(f32[16,4,128,1,128]{2,4,3,1,0:T(8,128)} %get-tuple-element.42) | data formatting | bytes 8388608
  158.9 4.9 %add_convert_fusion.1 = (bf16[16,4,128,1,128]{4,0,3,2,1:T(8,128)(2,1)S(1)}, bf16[16,4,128,1,128]{4,0,3,2,1:T(8,128)(2,1)S(1)}) fusion(f32[16,4,128,1,128]{4,0,3,2,1:T(8,128)} %copy.85, f32[16,4,128,1,128]{4,0,3,2,1:T(8,128)} %copy.84, f32[16,128,128]{2,0,1:T(8,128)} %get-tuple-element.44, f32[16,128,128]{2,0,1:T(8,128)S(1)} %get-tuple-element.43), kind=kLoop, calls=%fused_computation.9 | loop fusion | flops 8388608 | bytes 14680064 | tf_op jit(solution)/shard_map/convert.8
  163.8 0.4 pad_maximum_fusion
  164.2 6.6 %copy.67 = bf16[16,4,128,2,128]{4,3,2,1,0:T(2,128)(2,1)} copy(bf16[16,4,128,2,128]{4,0,3,2,1:T(8,128)(2,1)S(1)} %pad_maximum_fusion) | data formatting | bytes 8388608 | tf_op jit(solution)/shard_map/while/body/eval_jaxpr/stack | solution.py:52
  170.8 7.8 %convert_element_type.145 = bf16[64,32768]{1,0:T(8,128)(2,1)} reshape(bf16[16,4,128,2,128]{4,3,2,1,0:T(2,128)(2,1)} %copy.67) | data formatting | bytes 8388608 | tf_op jit(solution)/shard_map/while/body/eval_jaxpr/convert_element_type | solution.py:55
  178.6 3.7 fusion.37
  182.3 0.1 reduce_sum.18
  182.4 0.1 reduce_sum.19
  182.6 0.1 div.67
  182.6 0.1 div.68
  182.7 0.1 copy.70
  182.9 2.4 fusion.6
  185.2 1.5 subtract_convert_fusion
  186.8 0.4 pad_maximum_fusion.1
  187.1 6.6 %copy.72 = bf16[16,4,128,2,128]{4,3,2,1,0:T(2,128)(2,1)} copy(bf16[16,4,128,2,128]{4,0,3,2,1:T(8,128)(2,1)S(1)} %pad_maximum_fusion.1) | data formatting | bytes 8388608 | tf_op jit(solution)/shard_map/while/body/eval_jaxpr/stack | solution.py:65
  193.7 7.8 %convert_element_type.150 = bf16[64,32768]{1,0:T(8,128)(2,1)} reshape(bf16[16,4,128,2,128]{4,3,2,1,0:T(2,128)(2,1)} %copy.72) | data formatting | bytes 8388608 | tf_op jit(solution)/shard_map/while/body/eval_jaxpr/convert_element_type | solution.py:68
  201.5 3.4 fusion
  205.0 8.1 %copy.74 = f32[64,128,256]{2,1,0:T(8,128)} copy(f32[64,128,256]{2,0,1:T(8,128)S(1)} %fusion) | data formatting | bytes 16777216 | tf_op jit(solution)/shard_map/dot_general | solution.py:121
  213.0 0.0 reduce-scatter.2.cloned.1.call-update
  213.1 0.0 all-reduce.2.cloned.1.call-start
  213.1 149.0 %reduce-scatter.2.cloned.1.call-done = f32[1,128,256]{2,1,0:T(8,128)} async-done(((f32[64,128,256]{2,1,0:T(8,128)}), f32[1,128,256]{2,1,0:T(8,128)}) %reduce-scatter.2.cloned.1.call-update) | async-done | bytes 131088 | tf_op jit(solution)/shard_map/reduce_scatter | solution.py:124
  362.1 0.9 convert_element_type.151
  363.0 0.3 fusion.3
  363.4 0.3 copy.76
  363.7 24.8 %all_to_all.10 = bf16[64,16,256]{2,1,0:T(8,128)(2,1)S(1)} all-to-all(bf16[64,16,256]{2,1,0:T(8,128)(2,1)S(1)} %copy.76), channel_id=1, replica_groups=mesh['slab'=64,'img'=4] {'slab'}, dimensions={0} | all-to-all | bytes 1048576 | tf_op jit(solution)/shard_map/all_to_all | solution.py:133
  388.5 1.2 convolution_bitcast_fusion
  389.7 0.0 all-reduce.2.cloned.1.call-update
  389.8 0.1 copy.77
  389.9 0.1 mul.346
  389.9 0.7 broadcast_divide_fusion
  390.6 45.1 %all-reduce.2.cloned.1.call-done = f32[512,256]{0,1:T(8,128)} async-done(((f32[512,256]{0,1:T(8,128)}), f32[512,256]{0,1:T(8,128)}) %all-reduce.2.cloned.1.call-update) | async-done | bytes 524304 | tf_op jit(solution)/shard_map/psum | solution.py:135
  435.7 1.1 broadcast_multiply_fusion
  436.8 1.0 copy.78
  (18 shorter events, 0.1 us)
Async XLA Ops:
  7.2 1.2 copy-start
  7.2 44.7 %copy-start.4 = (s32[1,16,4]{1,2,0:T(4,128)S(1)}, s32[1,16,4]{1,2,0:T(4,128)}, u32[]{:S(2)}) copy-start(s32[1,16,4]{1,2,0:T(4,128)} %param.11) | copy-start | bytes 772
  10.8 39.2 %all-to-all-start = ((f32[64,16,256]{2,1,0:T(8,128)}), f32[64,16,256]{2,1,0:T(8,128)S(1)}, u32[]{:S(2)}, u32[]{:S(2)}) async-start(f32[64,16,256]{2,1,0:T(8,128)} %fusion.10), calls=%async_computation | async-start | bytes 2097152 | tf_op jit(solution)/shard_map/all_to_all | solution.py:85
  22.8 105.4 %all-gather.2.cloned.1.call-start = ((), (), s32[]{:S(2)}) async-start(), calls=%async_computation.3 | async-start | bytes 4259840 | tf_op jit(solution)/shard_map/all_gather | solution.py:100
  51.6 310.5 %reduce-scatter.2.cloned.1.call-start = ((), (), s32[]{:S(2)}) async-start(), calls=%async_computation.4 | async-start | bytes 8519680 | tf_op jit(solution)/shard_map/reduce_scatter | solution.py:124
  54.2 11.1 %copy-start.5 = (f32[1,16]{1,0:T(1,128)S(1)}, f32[1,16]{1,0:T(1,128)}, u32[]{:S(2)}) copy-start(f32[1,16]{1,0:T(1,128)} %param.10) | copy-start | bytes 196
  59.8 0.8 copy-start.2
  178.6 4.3 copy-start.3
  182.9 2.4 copy-start.1
  213.1 222.6 %all-reduce.2.cloned.1.call-start = ((), (), s32[]{:S(2)}) async-start(), calls=%async_computation.5 | async-start | bytes 1048576 | tf_op jit(solution)/shard_map/psum | solution.py:135
Sparse Core Ops, SparseCore 0:
  51.7 76.3 all-gather.1
  213.2 148.8 reduce-scatter.1
  389.9 45.7 all-reduce.1
where the time goes:
time: 445 us; the launch traced here: 444 us
  waiting for transfers between devices  277 us (62%)
  local copies, waits for them, and re-layouts  80.9 us (18%)
  blocking collectives  24.8 us (6%)
  other arithmetic  20.7 us (5%)
  matrix products  14.5 us (3%)
  between operations  14 us (3%)
  starting transfers between devices  12.3 us (3%)
    reduce_scatter x1, waiting for transfers between devices, on_device(): lax.psum_scatter(contrib, 'slab', scatter_dimension=0, tiled=True)  149 us
    all_gather x1, waiting for transfers between devices, on_device(): lax.all_gather(summed.astype(jnp.bfloat16), 'slab', axis=0, tiled=True)  56.5 us
    psum x1, waiting for transfers between devices, on_device(): summed_cols = lax.psum(column, 'img')  45.1 us
    all_to_all x1, waiting for transfers between devices, on_device(): lax.all_to_all(partial_value.reshape(slab_count, ori_dev * block_rows, 2...  26.4 us
    all_to_all x1, blocking collectives, on_device(): lax.all_to_all(outgoing, 'slab', split_axis=0, concat_axis=0, tiled=True)  24.8 us
    unnamed x16, local copies, waits for them, and re-layouts  14.1 us
    all_to_all x1, starting transfers between devices, on_device(): lax.all_to_all(partial_value.reshape(slab_count, ori_dev * block_rows, 2...  12 us
    another operation x3, other arithmetic  11.8 us
  transfers between devices with their start and end apart: 4, of which 4 were waited for; matrix products, arithmetic and copies ran while one was open for 5% of the time, Pallas kernels for 0%

commit v1 on v0

--- a/solution.py
+++ b/solution.py
@@ -132,7 +132,11 @@
     outgoing = outgoing.astype(jnp.bfloat16).reshape(slab_count * ori_dev, block_rows, 2 * fourier)
     incoming = lax.all_to_all(outgoing, "slab", split_axis=0, concat_axis=0, tiled=True)
     column = jnp.einsum("jpr,jpx->rx", interp[0], incoming, preferred_element_type=jnp.float32)
-    summed_cols = lax.psum(column, "img")
+    summed_cols = column
+    for hop in (1, 2):
+        summed_cols = summed_cols + lax.ppermute(
+            summed_cols, "img", [(dev, dev ^ hop) for dev in range(4)]
+        )
     update = summed_cols / math.sqrt(img_dev * slab_count)
     return (update, weights)
 

time: 445 us -> 428 us (0.962)
  waiting for transfers between devices: 277 us -> 256 us
  starting transfers between devices: 12.3 us -> 17 us
    psum x1 -> x0, waiting for transfers between devices: 45.1 us -> none  [on_device(): summed_cols = lax.psum(column, 'img')]
    ppermute x0 -> x2, waiting for transfers between devices: none -> 24.3 us  [on_device(): lax.ppermute(summed_cols, 'img', [(dev, dev ^ hop) for dev in range(4)])]
    ppermute x0 -> x2, starting transfers between devices: none -> 4.67 us  [on_device(): lax.ppermute(summed_cols, 'img', [(dev, dev ^ hop) for dev in range(4)])]
  transfers between devices with their start and end apart: 4 -> 5, of which waited for: 4 -> 5; matrix products, arithmetic and copies ran while one was open for 5% -> 5% of each run, Pallas kernels for 0% -> 0%
where the time goes in v1:
time: 428 us; the launch traced here: 427 us
  waiting for transfers between devices  256 us (60%)
  local copies, waits for them, and re-layouts  81.1 us (19%)
  blocking collectives  24.8 us (6%)
  other arithmetic  19.8 us (5%)
  starting transfers between devices  17 us (4%)
  between operations  14.3 us (3%)
  matrix products  13.7 us (3%)
    reduce_scatter x1, waiting for transfers between devices, on_device(): lax.psum_scatter(contrib, 'slab', scatter_dimension=0, tiled=True)  149 us
    all_gather x1, waiting for transfers between devices, on_device(): lax.all_gather(summed.astype(jnp.bfloat16), 'slab', axis=0, tiled=True)  56.5 us
    all_to_all x1, waiting for transfers between devices, on_device(): lax.all_to_all(partial_value.reshape(slab_count, ori_dev * block_rows, 2...  26.4 us
    all_to_all x1, blocking collectives, on_device(): lax.all_to_all(outgoing, 'slab', split_axis=0, concat_axis=0, tiled=True)  24.8 us
    ppermute x2, waiting for transfers between devices, on_device(): lax.ppermute(summed_cols, 'img', [(dev, dev ^ hop) for dev in range(4)])  24.3 us
    unnamed x16, local copies, waits for them, and re-layouts  14.1 us
    all_to_all x1, starting transfers between devices, on_device(): lax.all_to_all(partial_value.reshape(slab_count, ori_dev * block_rows, 2...  12 us
    another operation x3, other arithmetic  11.8 us
  transfers between devices with their start and end apart: 5, of which 5 were waited for; matrix products, arithmetic and copies ran while one was open for 5% of the time, Pallas kernels for 0%

profile of v1, /device:TPU:2, one launch (start us, length us, event | category | flops | bytes accessed | tf_op | source)
XLA Modules:
  0.0 426.8 jit_solution(9064254444183800111)
XLA Ops:
  7.2 1.2 copy-done
  8.4 2.4 fusion.10
  10.8 12.0 %all-to-all-start = ((f32[64,16,256]{2,1,0:T(8,128)}), f32[64,16,256]{2,1,0:T(8,128)S(1)}, u32[]{:S(2)}, u32[]{:S(2)}) async-start(f32[64,16,256]{2,1,0:T(8,128)} %fusion.10), calls=%async_computation | async-start | bytes 2097152 | tf_op jit(solution)/shard_map/all_to_all | solution.py:85
  22.8 0.0 all-gather.2.cloned.1.call-start
  22.8 0.7 dynamic-slice_bitcast_fusion
  23.5 26.4 %all-to-all-done = f32[64,16,256]{2,1,0:T(8,128)S(1)} async-done(((f32[64,16,256]{2,1,0:T(8,128)}), f32[64,16,256]{2,1,0:T(8,128)S(1)}, u32[]{:S(2)}, u32[]{:S(2)}) %all-to-all-start) | async-done | bytes 1048608 | tf_op jit(solution)/shard_map/all_to_all | solution.py:85
  49.9 1.0 convolution_convert_fusion.1
  51.0 0.6 copy.62
  51.6 0.2 reduce-scatter.2.cloned.1.call-start
  51.9 0.1 copy.57
  52.0 0.1 copy.63
  52.0 0.1 reshape.434
  52.1 2.1 reshape.430
  54.3 0.1 broadcast_multiply_fusion.1
  54.3 0.1 copy.68
  54.4 5.4 %fusion.14 = (bf16[128,1,128,16]{2,3,1,0:T(8,128)(2,1)S(1)}, bf16[128,1,128,16]{2,3,1,0:T(8,128)(2,1)}, bf16[128,1,128,16]{2,3,1,0:T(8,128)(2,1)S(1)}) fusion(f32[128,16]{0,1:T(8,128)S(1)} %get-tuple-element.51, f32[128,16]{1,0:T(8,128)S(1)} %copy.68), kind=kLoop, calls=%fused_computation.32 | loop fusion | flops 1572864 | bytes 1589248 | tf_op jit(solution)/shard_map/convert.7
  59.8 0.8 copy-done.2
  60.6 0.1 pad_maximum_fusion.3
  60.7 1.9 copy.69
  62.6 2.6 convert_element_type.148
  65.3 0.1 eq.65
  65.4 0.1 add_multiply_fusion.3
  65.5 3.9 add_negate_fusion
  69.4 1.2 copy_multiply_fusion
  70.6 1.1 slice_bitcast_fusion.1
  71.7 56.5 %all-gather.2.cloned.1.call-done = bf16[64,128,256]{2,1,0:T(8,128)(2,1)} async-done(((bf16[1,128,256]{2,1,0:T(8,128)(2,1)}), bf16[64,128,256]{2,1,0:T(8,128)(2,1)}) %all-gather.2.cloned.1.call-update) | async-done | bytes 4194320 | tf_op jit(solution)/shard_map/all_gather | solution.py:100
  128.2 5.0 %gather_fusion = bf16[64,128,256]{2,1,0:T(8,128)(2,1)} fusion(bf16[64,128,256]{2,1,0:T(8,128)(2,1)} %all-gather.2.cloned.1.call-done, s32[1024]{0:T(1024)S(1)} %pad_clamp_fusion), kind=kCustom, calls=%fused_computation | custom fusion | bytes 8388864 | tf_op jit(solution)/shard_map/while/body/eval_jaxpr/gather | solution.py:49
  133.2 7.0 %copy.64 = f32[64,128,256]{1,2,0:T(8,128)} copy(bf16[64,128,256]{2,1,0:T(8,128)(2,1)} %gather_fusion) | data formatting | bytes 12582912 | tf_op jit(solution)/shard_map/while/body/eval_jaxpr/convert_element_type | solution.py:49
  140.2 7.8 %fusion.36 = (f32[16,4,128,1,128]{2,4,3,1,0:T(8,128)}, f32[16,4,128,1,128]{2,4,3,1,0:T(8,128)}) fusion(f32[16,4,128,2,128]{2,4,3,1,0:T(8,128)} %bitcast.62), kind=kLoop, calls=%fused_computation.73 | loop fusion | bytes 16777216 | tf_op jit(solution)/shard_map/while/body/eval_jaxpr/slice | solution.py:50
  148.0 5.5 %copy.84 = f32[16,4,128,1,128]{4,0,3,2,1:T(8,128)} copy(f32[16,4,128,1,128]{2,4,3,1,0:T(8,128)} %get-tuple-element.41) | data formatting | bytes 8388608
  153.5 5.5 %copy.85 = f32[16,4,128,1,128]{4,0,3,2,1:T(8,128)} copy(f32[16,4,128,1,128]{2,4,3,1,0:T(8,128)} %get-tuple-element.42) | data formatting | bytes 8388608
  159.0 4.9 %add_convert_fusion.1 = (bf16[16,4,128,1,128]{4,0,3,2,1:T(8,128)(2,1)S(1)}, bf16[16,4,128,1,128]{4,0,3,2,1:T(8,128)(2,1)S(1)}) fusion(f32[16,4,128,1,128]{4,0,3,2,1:T(8,128)} %copy.85, f32[16,4,128,1,128]{4,0,3,2,1:T(8,128)} %copy.84, f32[16,128,128]{2,0,1:T(8,128)} %get-tuple-element.44, f32[16,128,128]{2,0,1:T(8,128)S(1)} %get-tuple-element.43), kind=kLoop, calls=%fused_computation.9 | loop fusion | flops 8388608 | bytes 14680064 | tf_op jit(solution)/shard_map/convert.8
  163.9 0.4 pad_maximum_fusion
  164.3 6.6 %copy.67 = bf16[16,4,128,2,128]{4,3,2,1,0:T(2,128)(2,1)} copy(bf16[16,4,128,2,128]{4,0,3,2,1:T(8,128)(2,1)S(1)} %pad_maximum_fusion) | data formatting | bytes 8388608 | tf_op jit(solution)/shard_map/while/body/eval_jaxpr/stack | solution.py:52
  170.9 7.8 %convert_element_type.145 = bf16[64,32768]{1,0:T(8,128)(2,1)} reshape(bf16[16,4,128,2,128]{4,3,2,1,0:T(2,128)(2,1)} %copy.67) | data formatting | bytes 8388608 | tf_op jit(solution)/shard_map/while/body/eval_jaxpr/convert_element_type | solution.py:55
  178.7 3.7 fusion.37
  182.5 0.1 reduce_sum.18
  182.5 0.1 reduce_sum.19
  182.7 0.1 div.67
  182.7 0.1 div.68
  182.9 0.1 copy.70
  183.0 2.3 fusion.6
  185.3 1.5 subtract_convert_fusion
  186.9 0.4 pad_maximum_fusion.1
  187.2 6.6 %copy.72 = bf16[16,4,128,2,128]{4,3,2,1,0:T(2,128)(2,1)} copy(bf16[16,4,128,2,128]{4,0,3,2,1:T(8,128)(2,1)S(1)} %pad_maximum_fusion.1) | data formatting | bytes 8388608 | tf_op jit(solution)/shard_map/while/body/eval_jaxpr/stack | solution.py:65
  193.8 7.9 %convert_element_type.150 = bf16[64,32768]{1,0:T(8,128)(2,1)} reshape(bf16[16,4,128,2,128]{4,3,2,1,0:T(2,128)(2,1)} %copy.72) | data formatting | bytes 8388608 | tf_op jit(solution)/shard_map/while/body/eval_jaxpr/convert_element_type | solution.py:68
  201.7 3.4 fusion
  205.1 8.1 %copy.74 = f32[64,128,256]{2,1,0:T(8,128)} copy(f32[64,128,256]{2,0,1:T(8,128)S(1)} %fusion) | data formatting | bytes 16777216 | tf_op jit(solution)/shard_map/dot_general | solution.py:121
  213.2 149.0 %reduce-scatter.2.cloned.1.call-done = f32[1,128,256]{2,1,0:T(8,128)} async-done(((f32[64,128,256]{2,1,0:T(8,128)}), f32[1,128,256]{2,1,0:T(8,128)}) %reduce-scatter.2.cloned.1.call-update) | async-done | bytes 131088 | tf_op jit(solution)/shard_map/reduce_scatter | solution.py:124
  362.2 0.9 convert_element_type.151
  363.1 0.3 fusion.3
  363.4 0.3 copy.76
  363.7 24.8 %all_to_all.10 = bf16[64,16,256]{2,1,0:T(8,128)(2,1)S(1)} all-to-all(bf16[64,16,256]{2,1,0:T(8,128)(2,1)S(1)} %copy.76), channel_id=1, replica_groups=mesh['slab'=64,'img'=4] {'slab'}, dimensions={0} | all-to-all | bytes 1048576 | tf_op jit(solution)/shard_map/all_to_all | solution.py:133
  388.6 0.4 convolution_bitcast_fusion
  389.0 1.6 collective-permute-start
  390.6 13.0 %collective-permute-done = f32[512,256]{0,1:T(8,128)S(1)} collective-permute-done((f32[512,256]{0,1:T(8,128)S(1)}, f32[512,256]{0,1:T(8,128)S(1)}, u32[]{:S(2)}, u32[]{:S(2)}) %collective-permute-start) | collective-permute-done | bytes 524320 | tf_op jit(solution)/shard_map/ppermute | solution.py:137
  403.5 0.1 add.191
  403.6 3.1 collective-permute-start.1
  406.7 0.1 copy.77
  406.8 0.1 mul.346
  406.9 0.7 broadcast_divide_fusion
  407.6 11.3 %collective-permute-done.1 = f32[512,256]{0,1:T(8,128)S(1)} collective-permute-done((f32[512,256]{0,1:T(8,128)S(1)}, f32[512,256]{0,1:T(8,128)S(1)}, u32[]{:S(2)}, u32[]{:S(2)}) %collective-permute-start.1) | collective-permute-done | bytes 524320 | tf_op jit(solution)/shard_map/ppermute | solution.py:137
  418.9 0.1 add_multiply_fusion.1
  419.0 1.0 copy.78
  (20 shorter events, 0.1 us)
Async XLA Ops:
  7.2 1.2 copy-start
  7.2 44.7 %copy-start.4 = (s32[1,16,4]{1,2,0:T(4,128)S(1)}, s32[1,16,4]{1,2,0:T(4,128)}, u32[]{:S(2)}) copy-start(s32[1,16,4]{1,2,0:T(4,128)} %param.11) | copy-start | bytes 772
  10.8 39.2 %all-to-all-start = ((f32[64,16,256]{2,1,0:T(8,128)}), f32[64,16,256]{2,1,0:T(8,128)S(1)}, u32[]{:S(2)}, u32[]{:S(2)}) async-start(f32[64,16,256]{2,1,0:T(8,128)} %fusion.10), calls=%async_computation | async-start | bytes 2097152 | tf_op jit(solution)/shard_map/all_to_all | solution.py:85
  22.8 105.4 %all-gather.2.cloned.1.call-start = ((), (), s32[]{:S(2)}) async-start(), calls=%async_computation.3 | async-start | bytes 4259840 | tf_op jit(solution)/shard_map/all_gather | solution.py:100
  51.6 310.6 %reduce-scatter.2.cloned.1.call-start = ((), (), s32[]{:S(2)}) async-start(), calls=%async_computation.4 | async-start | bytes 8519680 | tf_op jit(solution)/shard_map/reduce_scatter | solution.py:124
  54.2 11.2 %copy-start.5 = (f32[1,16]{1,0:T(1,128)S(1)}, f32[1,16]{1,0:T(1,128)}, u32[]{:S(2)}) copy-start(f32[1,16]{1,0:T(1,128)} %param.10) | copy-start | bytes 196
  59.8 0.8 copy-start.2
  178.7 4.3 copy-start.3
  183.0 2.4 copy-start.1
  389.0 14.5 %collective-permute-start = (f32[512,256]{0,1:T(8,128)S(1)}, f32[512,256]{0,1:T(8,128)S(1)}, u32[]{:S(2)}, u32[]{:S(2)}) collective-permute-start(f32[512,256]{0,1:T(8,128)S(1)} %convolution_bitcast_fusion), channel_id=1, source_target_pairs={{0,1},{1,0},{2,3},{3,2},{4,5},{5,4},{6,7},{7,6},{8,9},{9,8},{10,11... | collective-permute-start | bytes 1572872 | tf_op jit(solution)/shard_map/ppermute | solution.py:137
  403.6 15.3 %collective-permute-start.1 = (f32[512,256]{0,1:T(8,128)S(1)}, f32[512,256]{0,1:T(8,128)S(1)}, u32[]{:S(2)}, u32[]{:S(2)}) collective-permute-start(f32[512,256]{0,1:T(8,128)S(1)} %add.191), channel_id=1, source_target_pairs={{0,2},{1,3},{2,0},{3,1},{4,6},{5,7},{6,4},{7,5},{8,10},{9,11},{10,... | collective-permute-start | bytes 1572872 | tf_op jit(solution)/shard_map/ppermute | solution.py:137
Sparse Core Ops, SparseCore 0:
  51.7 76.3 all-gather.1
  213.3 148.7 reduce-scatter.1
